TPU v7x, 32 devices: a whole 2x2x4 slice. The times are simulated.
32 devices in a mesh: dp: 4 (over y, x), seq: 8 (over z, core).
Axes of the slice: x: 2, y: 2, z: 4, core: 2. Of those that a mesh axis runs over, the one named last changes fastest.
Arguments:
- tokens: bfloat16 [4, 4, 512, 1024], P('dp', None, 'seq'), may hold values from -6 to 6
- norm1_gain: bfloat16 [1024], P('dp'), may hold values from 0.5 to 1.5
- w_query: bfloat16 [1024, 1024], P('dp'), may hold values from -0.1875 to 0.1875
- w_latent: bfloat16 [1024, 512], P('dp'), may hold values from -0.1875 to 0.1875
- w_key_up: bfloat16 [256, 1024], P('dp'), may hold values from -0.375 to 0.375
- w_value_up: bfloat16 [256, 1024], P('dp'), may hold values from -0.375 to 0.375
- w_out: bfloat16 [1024, 1024], P('dp'), may hold values from -1.5 to 1.5
- norm2_gain: bfloat16 [1024], P('dp'), may hold values from 0.5 to 1.5
- w_gate: bfloat16 [1024, 2816], P('dp'), may hold values from -0.1875 to 0.1875
- w_up: bfloat16 [1024, 2816], P('dp'), may hold values from -0.1875 to 0.1875
- w_down: bfloat16 [2816, 1024], P('dp'), may hold values from -0.109375 to 0.109375
- out_grad: bfloat16 [4, 4, 512, 1024], P('dp', None, 'seq'), may hold values from -6 to 6
- seq_lengths: int32 [4, 66], P('dp'), may hold values from 0 to 1024, as said below
Outputs:
- layer_out: bfloat16 [4, 4, 512, 1024], P('dp', None, 'seq')
- tokens_grad: bfloat16 [4, 4, 512, 1024], P('dp', None, 'seq')
- norm1_gain_grad: float32 [1024], P('dp')
- w_query_grad: float32 [1024, 1024], P('dp')
- w_latent_grad: float32 [1024, 512], P('dp')
- w_key_up_grad: float32 [256, 1024], P('dp')
- w_value_up_grad: float32 [256, 1024], P('dp')
- w_out_grad: float32 [1024, 1024], P('dp')
- norm2_gain_grad: float32 [1024], P('dp')
- w_gate_grad: float32 [1024, 2816], P('dp')
- w_up_grad: float32 [1024, 2816], P('dp')
- w_down_grad: float32 [2816, 1024], P('dp')
Inputs may be any that keep to these rules, and one draw needn't show every extreme that they name: `seq_lengths`: the entries of a stream sum to 2048. Even entries are sequence lengths; every stream holds one sequence of exactly 1024 positions. Odd entries are padding of at most 64 positions.
All inputs are finite; a program needn't handle non-finite values.
Results may differ from a plain program's by a relative error of at most 0.02.
Values may be sent and summed in bfloat16 or wider, within the bound.
No kernel may reach another device: no remote copies, remote signals or barrier semaphores. Data moves between devices by JAX's collectives and lax.ppermute only.
A program may use at most 256 MiB of HBM per device.

v0:
```python
import math
import jax
import jax.numpy as jnp
from jax import lax
from jax.sharding import PartitionSpec as P

HEADS = 16
HEAD_DIM = 64
GROUPS = 2
LATENT = 256
SEQ_MIN = 1024
NEG_FILL = -1e30
NORM_EPS = 1e-05


def rms_scale(values, gain):
    inverse = lax.rsqrt(jnp.mean(values * values, axis=-1, keepdims=True) + NORM_EPS)
    return values * inverse * gain


def swish_product(gate_vals, up_vals):
    return gate_vals * jax.nn.sigmoid(gate_vals) * up_vals


def seq_table(stretches):
    run_ends = jnp.cumsum(stretches)
    firsts = run_ends - stretches
    return (firsts[0::2], stretches[0::2])


def inside_table(starts, lengths, positions):
    return (positions[:, None] >= starts[None, :]) & (
        positions[:, None] < starts[None, :] + lengths[None, :]
    )


def label_rows(inside):
    labels = jnp.arange(1, inside.shape[1] + 1, dtype=jnp.int32)
    return jnp.sum(jnp.where(inside, labels[None, :], 0), axis=1)


def per_device(
    tokens,
    norm1_gain,
    w_query,
    w_latent,
    w_key_up,
    w_value_up,
    w_out,
    norm2_gain,
    w_gate,
    w_up,
    w_down,
    out_grad,
    seq_lengths,
):
    gathered = (
        lax.all_gather(norm1_gain, "dp", axis=0, tiled=True),
        lax.all_gather(w_query, "dp", axis=0, tiled=True),
        lax.all_gather(w_latent, "dp", axis=0, tiled=True),
        lax.all_gather(w_key_up, "dp", axis=0, tiled=True),
        lax.all_gather(w_value_up, "dp", axis=0, tiled=True),
        lax.all_gather(w_out, "dp", axis=0, tiled=True),
        lax.all_gather(norm2_gain, "dp", axis=0, tiled=True),
        lax.all_gather(w_gate, "dp", axis=0, tiled=True),
        lax.all_gather(w_up, "dp", axis=0, tiled=True),
        lax.all_gather(w_down, "dp", axis=0, tiled=True),
    )
    gain_one, query_w, latent_w, key_w, value_w, out_w, gain_two, gate_w, up_w, down_w = gathered
    piece_count = tokens.shape[1]
    block_rows = tokens.shape[2]
    row_width = tokens.shape[3]
    tok_rows = piece_count * block_rows
    my_index = lax.axis_index("seq")
    span_rows = block_rows * lax.axis_size("seq")
    longest = max(SEQ_MIN, span_rows)
    window = longest + block_rows
    stream_len = piece_count * span_rows
    latent_width = GROUPS * LATENT
    per_group = HEADS // GROUPS
    score_scale = 1.0 / math.sqrt(HEAD_DIM)
    seq_first, seq_len = seq_table(seq_lengths[0])
    row_pos = (
        jnp.arange(piece_count, dtype=jnp.int32)[:, None] * span_rows
        + my_index * block_rows
        + jnp.arange(block_rows, dtype=jnp.int32)[None, :]
    )
    row_labels = label_rows(inside_table(seq_first, seq_len, row_pos.reshape(-1))).reshape(
        piece_count, block_rows
    )
    key_first = jnp.maximum(row_pos[:, 0] + block_rows - window, 0)
    key_pos = key_first[:, None] + jnp.arange(window, dtype=jnp.int32)[None, :]
    key_labels = label_rows(inside_table(seq_first, seq_len, key_pos.reshape(-1))).reshape(
        piece_count, window
    )
    same_seq = (
        (row_labels[:, :, None] == key_labels[:, None, :])
        & (row_labels[:, :, None] > 0)
        & (key_pos[:, None, :] <= row_pos[:, :, None])
    )
    masks = same_seq | (key_pos[:, None, :] == row_pos[:, :, None])

    def windows_of(stream_vals):
        return jnp.stack(
            [
                lax.dynamic_slice_in_dim(stream_vals, key_first[piece_id], window, 0)
                for piece_id in range(piece_count)
            ]
        )

    tok_float = tokens[0].reshape(tok_rows, row_width).astype(jnp.float32)
    gain_one_f = gain_one.astype(jnp.float32)
    gain_two_f = gain_two.astype(jnp.float32)
    normed = rms_scale(tok_float, gain_one_f).astype(jnp.bfloat16)
    queries = jnp.dot(normed, query_w, preferred_element_type=jnp.float32).astype(jnp.bfloat16)
    latent = jnp.dot(normed, latent_w, preferred_element_type=jnp.float32).astype(jnp.bfloat16)
    key_up = key_w.reshape(LATENT, HEADS, HEAD_DIM)
    value_up = value_w.reshape(LATENT, HEADS, HEAD_DIM)
    query_heads = queries.reshape(tok_rows, HEADS, HEAD_DIM)
    absorbed = jnp.einsum(
        "thd,chd->thc", query_heads, key_up, preferred_element_type=jnp.float32
    ).astype(jnp.bfloat16)
    absorbed_p = absorbed.reshape(piece_count, block_rows, HEADS, LATENT)
    latent_pieces = latent.reshape(piece_count, block_rows, latent_width)
    whole_stream = lax.all_gather(latent_pieces, "seq", axis=1, tiled=True).reshape(
        stream_len, latent_width
    )
    key_blocks = windows_of(whole_stream)

    def group_scores(keys_p, group_id):
        head_span = slice(group_id * per_group, (group_id + 1) * per_group)
        group_queries = absorbed_p[:, :, head_span, :]
        group_keys = keys_p[:, :, group_id * LATENT : (group_id + 1) * LATENT]
        scores = (
            jnp.einsum(
                "pthc,pkc->pthk", group_queries, group_keys, preferred_element_type=jnp.float32
            )
            * score_scale
        )
        return (group_queries, group_keys, jnp.where(masks[:, :, None, :], scores, NEG_FILL))

    log_parts = []
    mixed_parts = []
    for group_id in range(GROUPS):
        group_keys, scores = group_scores(key_blocks, group_id)[1:]
        row_top = jnp.max(scores, axis=-1)
        group_log = row_top + jnp.log(jnp.sum(jnp.exp(scores - row_top[..., None]), axis=-1))
        prob_vals = jnp.exp(scores - group_log[..., None]).astype(jnp.bfloat16)
        mixed_parts.append(
            jnp.einsum("pthk,pkc->pthc", prob_vals, group_keys, preferred_element_type=jnp.float32)
        )
        log_parts.append(group_log)
    log_total = jnp.concatenate(log_parts, axis=2)
    mixed_latent = jnp.concatenate(mixed_parts, axis=2).reshape(tok_rows, HEADS, LATENT)
    mixed_round = mixed_latent.astype(jnp.bfloat16)
    heads_out = (
        jnp.einsum("thc,chd->thd", mixed_round, value_up, preferred_element_type=jnp.float32)
        .astype(jnp.bfloat16)
        .reshape(tok_rows, HEADS * HEAD_DIM)
    )
    resid = tok_float + jnp.dot(heads_out, out_w, preferred_element_type=jnp.float32)
    normed_two = rms_scale(resid, gain_two_f).astype(jnp.bfloat16)
    gate_vals = jnp.dot(normed_two, gate_w, preferred_element_type=jnp.float32)
    up_vals = jnp.dot(normed_two, up_w, preferred_element_type=jnp.float32)
    hidden = swish_product(gate_vals, up_vals).astype(jnp.bfloat16)
    layer_out = (resid + jnp.dot(hidden, down_w, preferred_element_type=jnp.float32)).astype(
        jnp.bfloat16
    )
    grad_round = out_grad[0].reshape(tok_rows, row_width)
    grad_float = grad_round.astype(jnp.float32)
    down_grad = jnp.einsum("tf,td->fd", hidden, grad_round, preferred_element_type=jnp.float32)
    d_hidden = jnp.einsum("td,fd->tf", grad_round, down_w, preferred_element_type=jnp.float32)
    swish_pull = jax.vjp(swish_product, gate_vals, up_vals)[1]
    d_gate, d_up = swish_pull(d_hidden)
    d_gate = d_gate.astype(jnp.bfloat16)
    d_up = d_up.astype(jnp.bfloat16)
    gate_grad = jnp.einsum("td,tf->df", normed_two, d_gate, preferred_element_type=jnp.float32)
    up_grad = jnp.einsum("td,tf->df", normed_two, d_up, preferred_element_type=jnp.float32)
    d_normed_two = jnp.einsum(
        "tf,df->td", d_gate, gate_w, preferred_element_type=jnp.float32
    ) + jnp.einsum("tf,df->td", d_up, up_w, preferred_element_type=jnp.float32)
    norm_two_pull = jax.vjp(rms_scale, resid, gain_two_f)[1]
    d_resid_norm, gain_two_grad = norm_two_pull(d_normed_two)
    d_resid = grad_float + d_resid_norm
    d_resid_round = d_resid.astype(jnp.bfloat16)
    out_w_grad = jnp.einsum(
        "te,td->ed", heads_out, d_resid_round, preferred_element_type=jnp.float32
    )
    d_heads = (
        jnp.einsum("td,ed->te", d_resid_round, out_w, preferred_element_type=jnp.float32)
        .astype(jnp.bfloat16)
        .reshape(tok_rows, HEADS, HEAD_DIM)
    )
    value_grad = jnp.einsum(
        "thc,thd->chd", mixed_round, d_heads, preferred_element_type=jnp.float32
    ).reshape(LATENT, HEADS * HEAD_DIM)
    d_mixed = jnp.einsum(
        "thd,chd->thc", d_heads, value_up, preferred_element_type=jnp.float32
    ).astype(jnp.bfloat16)
    delta = jnp.sum(d_mixed.astype(jnp.float32) * mixed_latent, axis=-1)
    d_mixed_p = d_mixed.reshape(piece_count, block_rows, HEADS, LATENT)
    delta_p = delta.reshape(piece_count, block_rows, HEADS)
    again_stream = lax.all_gather(latent_pieces, "seq", axis=1, tiled=True).reshape(
        stream_len, latent_width
    )
    back_blocks = windows_of(again_stream)
    absorbed_parts = []
    key_parts = []
    for group_id in range(GROUPS):
        head_span = slice(group_id * per_group, (group_id + 1) * per_group)
        group_queries, group_keys, scores = group_scores(back_blocks, group_id)
        prob_vals = jnp.exp(scores - log_total[:, :, head_span, None])
        group_grads = d_mixed_p[:, :, head_span, :]
        d_probs = jnp.einsum(
            "pthc,pkc->pthk", group_grads, group_keys, preferred_element_type=jnp.float32
        )
        d_scores = (prob_vals * (d_probs - delta_p[:, :, head_span, None])).astype(jnp.bfloat16)
        absorbed_parts.append(
            jnp.einsum("pthk,pkc->pthc", d_scores, group_keys, preferred_element_type=jnp.float32)
        )
        key_terms = score_scale * jnp.einsum(
            "pthk,pthc->pkc", d_scores, group_queries, preferred_element_type=jnp.float32
        )
        key_terms = key_terms + jnp.einsum(
            "pthk,pthc->pkc",
            prob_vals.astype(jnp.bfloat16),
            group_grads,
            preferred_element_type=jnp.float32,
        )
        key_parts.append(key_terms)
    d_abs_sum = jnp.concatenate(absorbed_parts, axis=2).reshape(tok_rows, HEADS, LATENT)
    window_grads = jnp.concatenate(key_parts, axis=2)
    grad_term = jnp.zeros((stream_len, latent_width), jnp.float32)
    for piece_id in range(piece_count):
        current = lax.dynamic_slice_in_dim(grad_term, key_first[piece_id], window, 0)
        grad_term = lax.dynamic_update_slice_in_dim(
            grad_term, current + window_grads[piece_id], key_first[piece_id], 0
        )
    latent_total = lax.psum_scatter(
        grad_term.reshape(piece_count, span_rows, latent_width),
        "seq",
        scatter_dimension=1,
        tiled=True,
    ).reshape(tok_rows, latent_width)
    d_absorbed = (score_scale * d_abs_sum).astype(jnp.bfloat16)
    key_grad = jnp.einsum(
        "thc,thd->chd", d_absorbed, query_heads, preferred_element_type=jnp.float32
    ).reshape(LATENT, HEADS * HEAD_DIM)
    d_queries = (
        jnp.einsum("thc,chd->thd", d_absorbed, key_up, preferred_element_type=jnp.float32)
        .astype(jnp.bfloat16)
        .reshape(tok_rows, HEADS * HEAD_DIM)
    )
    d_latent = latent_total.astype(jnp.bfloat16)
    query_grad = jnp.einsum("td,te->de", normed, d_queries, preferred_element_type=jnp.float32)
    latent_grad = jnp.einsum("td,te->de", normed, d_latent, preferred_element_type=jnp.float32)
    d_normed = jnp.einsum(
        "te,de->td", d_queries, query_w, preferred_element_type=jnp.float32
    ) + jnp.einsum("te,de->td", d_latent, latent_w, preferred_element_type=jnp.float32)
    norm_one_pull = jax.vjp(rms_scale, tok_float, gain_one_f)[1]
    d_tok_norm, gain_one_grad = norm_one_pull(d_normed)
    tokens_grad = (d_resid + d_tok_norm).astype(jnp.bfloat16)
    grads = (
        gain_one_grad,
        query_grad,
        latent_grad,
        key_grad,
        value_grad,
        out_w_grad,
        gain_two_grad,
        gate_grad,
        up_grad,
        down_grad,
    )
    shares = (
        lax.psum_scatter(
            grads[0].astype(jnp.bfloat16), "dp", scatter_dimension=0, tiled=True
        ).astype(jnp.float32),
        lax.psum_scatter(
            grads[1].astype(jnp.bfloat16), "dp", scatter_dimension=0, tiled=True
        ).astype(jnp.float32),
        lax.psum_scatter(
            grads[2].astype(jnp.bfloat16), "dp", scatter_dimension=0, tiled=True
        ).astype(jnp.float32),
        lax.psum_scatter(
            grads[3].astype(jnp.bfloat16), "dp", scatter_dimension=0, tiled=True
        ).astype(jnp.float32),
        lax.psum_scatter(
            grads[4].astype(jnp.bfloat16), "dp", scatter_dimension=0, tiled=True
        ).astype(jnp.float32),
        lax.psum_scatter(
            grads[5].astype(jnp.bfloat16), "dp", scatter_dimension=0, tiled=True
        ).astype(jnp.float32),
        lax.psum_scatter(
            grads[6].astype(jnp.bfloat16), "dp", scatter_dimension=0, tiled=True
        ).astype(jnp.float32),
        lax.psum_scatter(
            grads[7].astype(jnp.bfloat16), "dp", scatter_dimension=0, tiled=True
        ).astype(jnp.float32),
        lax.psum_scatter(
            grads[8].astype(jnp.bfloat16), "dp", scatter_dimension=0, tiled=True
        ).astype(jnp.float32),
        lax.psum_scatter(
            grads[9].astype(jnp.bfloat16), "dp", scatter_dimension=0, tiled=True
        ).astype(jnp.float32),
    )
    summed = lax.psum(
        (
            shares[0],
            shares[1],
            shares[2],
            shares[3],
            shares[4],
            shares[5],
            shares[6],
            shares[7],
            shares[8],
            shares[9],
        ),
        "seq",
    )
    return (
        layer_out.reshape(1, piece_count, block_rows, row_width),
        tokens_grad.reshape(1, piece_count, block_rows, row_width),
        summed[0],
        summed[1],
        summed[2],
        summed[3],
        summed[4],
        summed[5],
        summed[6],
        summed[7],
        summed[8],
        summed[9],
    )


def solution(mesh):
    in_specs = (
        P("dp", None, "seq", None),
        P("dp"),
        P("dp", None),
        P("dp", None),
        P("dp", None),
        P("dp", None),
        P("dp", None),
        P("dp"),
        P("dp", None),
        P("dp", None),
        P("dp", None),
        P("dp", None, "seq", None),
        P("dp", None),
    )
    out_specs = (
        P("dp", None, "seq", None),
        P("dp", None, "seq", None),
        P("dp"),
        P("dp", None),
        P("dp", None),
        P("dp", None),
        P("dp", None),
        P("dp", None),
        P("dp"),
        P("dp", None),
        P("dp", None),
        P("dp", None),
    )
    return jax.shard_map(
        per_device, mesh=mesh, in_specs=in_specs, out_specs=out_specs, check_vma=False
    )
```

profile of v0, /device:TPU:0, one launch (start us, length us, event | category | flops | bytes accessed | tf_op | source)
XLA Modules:
  0.0 1120.6 jit_solution(5432038570921758720)
XLA Ops:
  11.3 9.5 all-gather
  22.1 17.1 %all-gather.12.cloned.1.call-done = bf16[1024,512]{1,0:T(8,128)(2,1)} async-done(((bf16[256,512]{1,0:T(8,128)(2,1)}), bf16[1024,512]{1,0:T(8,128)(2,1)}) %all-gather.12.cloned.1.call-update) | async-done | bytes 1048592 | tf_op jit(solution)/shard_map/all_gather | solution.py:60
  46.3 14.0 %all_gather.36 = bf16[256,1024]{1,0:T(8,128)(2,1)S(1)} all-gather(bf16[64,1024]{1,0:T(8,128)(2,1)S(1)} %copy-done.40), channel_id=1, replica_groups=mesh['dp'=4,'seq'=8] {'dp'}, dimensions={0}, use_global_device_ids=true | all-gather | bytes 655360 | tf_op jit(solution)/shard_map/all_gather | solution.py:61
  60.8 12.0 %all_gather.39 = bf16[256,1024]{1,0:T(8,128)(2,1)S(1)} all-gather(bf16[64,1024]{1,0:T(8,128)(2,1)S(1)} %copy-done.41), channel_id=1, replica_groups=mesh['dp'=4,'seq'=8] {'dp'}, dimensions={0}, use_global_device_ids=true | all-gather | bytes 655360 | tf_op jit(solution)/shard_map/all_gather | solution.py:62
  79.2 8.8 all-gather.1
  94.2 18.0 %all-gather.14.cloned.1.call-done = bf16[4,512,512]{2,1,0:T(8,128)(2,1)} async-done(((bf16[4,64,512]{2,1,0:T(8,128)(2,1)}), bf16[4,512,512]{2,1,0:T(8,128)(2,1)}) %all-gather.14.cloned.1.call-update) | async-done | bytes 2097168 | tf_op jit(solution)/shard_map/all_gather | solution.py:125
  112.2 3.6 dynamic-slice_bitcast_fusion.3
  116.5 3.1 fusion.67
  122.7 3.2 fusion.66
  128.9 3.4 fusion.32
  132.4 3.5 fusion.29
  140.6 8.2 all-gather.16.cloned.1.call-done
  151.4 64.9 %all-gather.18.cloned.1.call-done = bf16[1024,2816]{1,0:T(8,128)(2,1)} async-done(((bf16[256,2816]{1,0:T(8,128)(2,1)}), bf16[1024,2816]{1,0:T(8,128)(2,1)}) %all-gather.18.cloned.1.call-update) | async-done | bytes 5767184 | tf_op jit(solution)/shard_map/all_gather | solution.py:65
  216.3 5.9 fusion.68
  222.2 61.7 %all-gather.20.cloned.1.call-done = bf16[1024,2816]{1,0:T(8,128)(2,1)} async-done(((bf16[256,2816]{1,0:T(8,128)(2,1)}), bf16[1024,2816]{1,0:T(8,128)(2,1)}) %all-gather.20.cloned.1.call-update) | async-done | bytes 5767184 | tf_op jit(solution)/shard_map/all_gather | solution.py:66
  283.9 5.9 fusion.69
  289.7 61.8 %all-gather.22.cloned.1.call-done = bf16[2816,1024]{1,0:T(8,128)(2,1)} async-done(((bf16[704,1024]{1,0:T(8,128)(2,1)}), bf16[2816,1024]{1,0:T(8,128)(2,1)}) %all-gather.22.cloned.1.call-update) | async-done | bytes 5767184 | tf_op jit(solution)/shard_map/all_gather | solution.py:67
  351.5 9.5 multiply_convert_fusion.2
  361.1 5.4 fusion.70
  371.2 5.3 multiply_reduce_fusion
  377.9 6.8 multiply_convert_fusion
  386.9 4.0 fusion.49
  391.0 8.1 bitcast_add_fusion
  399.2 6.1 multiply_convert_fusion.1
  407.4 4.0 fusion.52
  411.4 7.5 bitcast_add_fusion.1
  424.5 6.7 dynamic_update_slice.12
  434.0 6.5 dynamic_update_slice.13
  443.3 6.5 dynamic_update_slice.14
  452.6 6.6 dynamic_update_slice.15
  459.2 4.5 convolution_convert_fusion.8
  464.9 4.7 fusion.55
  469.6 4.6 fusion.56
  485.7 23.7 %reduce-scatter.10.cloned.1.call-done = f32[4,64,512]{2,1,0:T(8,128)} async-done(((f32[4,512,512]{2,1,0:T(8,128)}), f32[4,64,512]{2,1,0:T(8,128)}) %reduce-scatter.10.cloned.1.call-update) | async-done | bytes 524304 | tf_op jit(solution)/shard_map/reduce_scatter | solution.py:239
  512.2 5.6 convolution_convert_fusion.2
  517.8 5.6 convolution_convert_fusion.1
  524.7 5.2 convolution_convert_fusion
  531.8 3.5 fusion.71
  535.3 5.6 fusion.21
  540.9 22.0 %reduce-scatter.16.cloned.1.call-done = bf16[64,1024]{1,0:T(8,128)(2,1)} async-done(((bf16[256,1024]{1,0:T(8,128)(2,1)}), bf16[64,1024]{1,0:T(8,128)(2,1)}) %reduce-scatter.16.cloned.1.call-update) | async-done | bytes 131088 | tf_op jit(solution)/shard_map/reduce_scatter | solution.py:285
  562.8 38.8 %reduce-scatter.20.cloned.1.call-done = bf16[256,1024]{1,0:T(8,128)(2,1)} async-done(((bf16[1024,1024]{1,0:T(8,128)(2,1)}), bf16[256,1024]{1,0:T(8,128)(2,1)}) %reduce-scatter.20.cloned.1.call-update) | async-done | bytes 524304 | tf_op jit(solution)/shard_map/reduce_scatter | solution.py:291
  601.6 38.9 %reduce-scatter.12.cloned.1.call-done = bf16[256,1024]{1,0:T(8,128)(2,1)} async-done(((bf16[1024,1024]{1,0:T(8,128)(2,1)}), bf16[256,1024]{1,0:T(8,128)(2,1)}) %reduce-scatter.12.cloned.1.call-update) | async-done | bytes 524304 | tf_op jit(solution)/shard_map/reduce_scatter | solution.py:279
  642.7 8.9 all-reduce.3
  652.8 18.3 %reduce-scatter.14.cloned.1.call-done = bf16[256,512]{1,0:T(8,128)(2,1)} async-done(((bf16[1024,512]{1,0:T(8,128)(2,1)}), bf16[256,512]{1,0:T(8,128)(2,1)}) %reduce-scatter.14.cloned.1.call-update) | async-done | bytes 262160 | tf_op jit(solution)/shard_map/reduce_scatter | solution.py:282
  671.1 69.0 %reduce-scatter.22.cloned.1.call-done = bf16[256,2816]{1,0:T(8,128)(2,1)} async-done(((bf16[1024,2816]{1,0:T(8,128)(2,1)}), bf16[256,2816]{1,0:T(8,128)(2,1)}) %reduce-scatter.22.cloned.1.call-update) | async-done | bytes 1441808 | tf_op jit(solution)/shard_map/reduce_scatter | solution.py:297
  740.1 68.9 %reduce-scatter.24.cloned.1.call-done = bf16[256,2816]{1,0:T(8,128)(2,1)} async-done(((bf16[1024,2816]{1,0:T(8,128)(2,1)}), bf16[256,2816]{1,0:T(8,128)(2,1)}) %reduce-scatter.24.cloned.1.call-update) | async-done | bytes 1441808 | tf_op jit(solution)/shard_map/reduce_scatter | solution.py:300
  809.1 68.9 %reduce-scatter.26.cloned.1.call-done = bf16[704,1024]{1,0:T(8,128)(2,1)} async-done(((bf16[2816,1024]{1,0:T(8,128)(2,1)}), bf16[704,1024]{1,0:T(8,128)(2,1)}) %reduce-scatter.26.cloned.1.call-update) | async-done | bytes 1441808 | tf_op jit(solution)/shard_map/reduce_scatter | solution.py:303
  878.0 235.7 %all-reduce.5 = (f32[256]{0:T(256)}, f32[256,1024]{1,0:T(8,128)}, f32[256,512]{1,0:T(8,128)}, f32[64,1024]{1,0:T(8,128)}, f32[64,1024]{1,0:T(8,128)}, /*index=5*...) all-reduce(f32[256]{0:T(256)S(1)} %get-tuple-element.60, ...), channel_id=1, replica_groups=mesh['dp'=4,'seq'=8] {'seq'}, use_global_device_ids=true, to_apply=%region_15.16 | all-reduce | flops 2949632 | bytes 17698816 | tf_op jit(solution)/shard_map/psum | solution.py:307
  (228 shorter events, 77.1 us)
Async XLA Ops:
  7.2 32.0 %all-gather.12.cloned.1.call-start = ((), (), s32[]{:S(2)}) async-start(), calls=%async_computation.10 | async-start | bytes 1310720 | tf_op jit(solution)/shard_map/all_gather | solution.py:60
  7.9 82.7 %all-gather.10.cloned.1.call-start = ((), (), s32[]{:S(2)}) async-start(), calls=%async_computation.9 | async-start | bytes 2621440 | tf_op jit(solution)/shard_map/all_gather | solution.py:59
  8.7 103.6 %all-gather.14.cloned.1.call-start = ((), (), s32[]{:S(2)}) async-start(), calls=%async_computation.11 | async-start | bytes 2359296 | tf_op jit(solution)/shard_map/all_gather | solution.py:125
  9.9 35.2 %copy-start.52 = (s32[1,66]{1,0:T(1,128)S(1)}, s32[1,66]{1,0:T(1,128)}, u32[]{:S(2)}) copy-start(s32[1,66]{1,0:T(1,128)} %param.25) | copy-start | bytes 796
  9.9 36.3 %copy-start.40 = (bf16[64,1024]{1,0:T(8,128)(2,1)S(1)}, bf16[64,1024]{1,0:T(8,128)(2,1)}, u32[]{:S(2)}) copy-start(bf16[64,1024]{1,0:T(8,128)(2,1)} %param.17) | copy-start | bytes 393220
  10.6 10.2 copy-start.48
  10.6 34.5 %copy-start.46 = (f32[256]{0:T(256)}, f32[256]{0:T(256)S(1)}, u32[]{:S(2)}) copy-start(f32[256]{0:T(256)S(1)} %rsqrt.25) | copy-start | bytes 3076
  20.8 24.3 %copy-start.44 = (f32[4,1,256]{2,1,0:T(1,128)}, f32[4,1,256]{2,1,0:T(1,128)S(1)}, u32[]{:S(2)}) copy-start(f32[4,1,256]{2,1,0:T(1,128)S(1)} %convert_element_type.250) | copy-start | bytes 12292
  22.1 38.7 %copy-start.41 = (bf16[64,1024]{1,0:T(8,128)(2,1)S(1)}, bf16[64,1024]{1,0:T(8,128)(2,1)}, u32[]{:S(2)}) copy-start(bf16[64,1024]{1,0:T(8,128)(2,1)} %param.18) | copy-start | bytes 393220
  41.6 107.2 %all-gather.16.cloned.1.call-start = ((), (), s32[]{:S(2)}) async-start(), calls=%async_computation.12 | async-start | bytes 2621440 | tf_op jit(solution)/shard_map/all_gather | solution.py:63
  42.2 37.0 %copy-start.54 = (bf16[256]{0:T(256)(128)(2,1)S(1)}, bf16[256]{0:T(256)(128)(2,1)}, u32[]{:S(2)}) copy-start(bf16[256]{0:T(256)(128)(2,1)} %param.20) | copy-start | bytes 1540
  42.2 174.1 %all-gather.18.cloned.1.call-start = ((), (), s32[]{:S(2)}) async-start(), calls=%async_computation.13 | async-start | bytes 7208960 | tf_op jit(solution)/shard_map/all_gather | solution.py:65
  42.8 241.1 %all-gather.20.cloned.1.call-start = ((), (), s32[]{:S(2)}) async-start(), calls=%async_computation.14 | async-start | bytes 7208960 | tf_op jit(solution)/shard_map/all_gather | solution.py:66
  43.4 308.2 %all-gather.22.cloned.1.call-start = ((), (), s32[]{:S(2)}) async-start(), calls=%async_computation.15 | async-start | bytes 7208960 | tf_op jit(solution)/shard_map/all_gather | solution.py:67
  44.1 465.2 %reduce-scatter.10.cloned.1.call-start = ((), (), s32[]{:S(2)}) async-start(), calls=%async_computation.16 | async-start | bytes 4718592 | tf_op jit(solution)/shard_map/reduce_scatter | solution.py:239
  78.2 15.9 %copy-start.29 = (bf16[256,1024]{0,1:T(8,128)(2,1)}, bf16[256,1024]{0,1:T(8,128)(2,1)S(1)}, u32[]{:S(2)}) copy-start(bf16[256,1024]{0,1:T(8,128)(2,1)S(1)} %copy.133) | copy-start | bytes 1572868
  93.3 22.6 %copy-start.21 = (bf16[256,1024]{0,1:T(8,128)(2,1)}, bf16[256,1024]{0,1:T(8,128)(2,1)S(1)}, u32[]{:S(2)}) copy-start(bf16[256,1024]{0,1:T(8,128)(2,1)S(1)} %copy.132) | copy-start | bytes 1572868
  94.2 22.3 %copy-start.36 = (bf16[4,64,8,256]{3,1,0,2:T(8,128)(2,1)}, bf16[4,64,8,256]{3,1,0,2:T(8,128)(2,1)S(1)}, u32[]{:S(2)}) copy-start(bf16[4,64,8,256]{3,1,0,2:T(8,128)(2,1)S(1)} %get-tuple-element.33) | copy-start | bytes 3145732
  94.2 28.5 %copy-start.38 = (bf16[4,64,8,256]{3,1,0,2:T(8,128)(2,1)}, bf16[4,64,8,256]{3,1,0,2:T(8,128)(2,1)S(1)}, u32[]{:S(2)}) copy-start(bf16[4,64,8,256]{3,1,0,2:T(8,128)(2,1)S(1)} %get-tuple-element.34) | copy-start | bytes 3145732
  119.7 9.3 copy-start
  135.9 12.9 %copy-start.5 = (bf16[1,4,64,1024]{3,2,1,0:T(8,128)(2,1)S(1)}, bf16[1,4,64,1024]{3,2,1,0:T(8,128)(2,1)}, u32[]{:S(2)}) copy-start(bf16[1,4,64,1024]{3,2,1,0:T(8,128)(2,1)} %param.13) | copy-start | bytes 1572868
  140.6 81.6 %copy-start.26 = (bf16[16,256,64]{1,2,0:T(8,128)(2,1)}, bf16[16,256,64]{1,2,0:T(8,128)(2,1)S(1)}, u32[]{:S(2)}) copy-start(bf16[16,256,64]{1,2,0:T(8,128)(2,1)S(1)} %convolution_convert_fusion.10) | copy-start | bytes 1572868
  151.2 217.6 %copy-start.11 = (f32[256,1024]{1,0:T(8,128)}, f32[256,1024]{1,0:T(8,128)S(1)}, u32[]{:S(2)}) copy-start(f32[256,1024]{1,0:T(8,128)S(1)} %get-tuple-element.54) | copy-start | bytes 3145732
  151.4 132.5 %copy-start.17 = (bf16[256,1024]{1,0:T(8,128)(2,1)}, bf16[256,1024]{1,0:T(8,128)(2,1)S(1)}, u32[]{:S(2)}) copy-start(bf16[256,1024]{1,0:T(8,128)(2,1)S(1)} %multiply_convert_fusion.4) | copy-start | bytes 1572868
  222.2 129.3 %copy-start.31 = (bf16[1,4,64,1024]{3,2,1,0:T(8,128)(2,1)S(1)}, bf16[1,4,64,1024]{3,2,1,0:T(8,128)(2,1)}, u32[]{:S(2)}) copy-start(bf16[1,4,64,1024]{3,2,1,0:T(8,128)(2,1)} %param.24) | copy-start | bytes 1572868
  377.7 7.0 copy-start.16
  377.9 9.0 copy-start.39
  386.9 12.2 %slice-start = ((s8[9437184]{0:T(1024)(128)(4,1)}), s8[4194304]{0:T(1024)(128)(4,1)S(1)}, s32[]{:S(2)}) async-start(s8[9437184]{0:T(1024)(128)(4,1)} %bitcast.166), calls=%async_computation.25 | async-start | bytes 8388608
  386.9 12.2 %slice-start.1 = ((s8[9437184]{0:T(1024)(128)(4,1)}), s8[4194304]{0:T(1024)(128)(4,1)S(1)}, s32[]{:S(2)}) async-start(s8[9437184]{0:T(1024)(128)(4,1)} %bitcast.166), calls=%async_computation.26 | async-start | bytes 8388608
  391.0 8.2 slice-start.2
  391.0 8.2 copy-start.32
  399.1 19.8 %copy-start.2 = (f32[4,1088,256]{2,1,0:T(8,128)}, f32[4,1088,256]{2,1,0:T(8,128)S(1)}, u32[]{:S(2)}) copy-start(f32[4,1088,256]{2,1,0:T(8,128)S(1)} %bitcast_add_fusion) | copy-start | bytes 13369348
  399.1 8.2 copy-start.37
  452.5 6.7 copy-start.20
  459.1 81.7 %reduce-scatter.18.cloned.1.call-start = ((), (), s32[]{:S(2)}) async-start(), calls=%async_computation.20 | async-start | bytes 655360 | tf_op jit(solution)/shard_map/reduce_scatter | solution.py:288
  464.8 98.0 %reduce-scatter.16.cloned.1.call-start = ((), (), s32[]{:S(2)}) async-start(), calls=%async_computation.19 | async-start | bytes 655360 | tf_op jit(solution)/shard_map/reduce_scatter | solution.py:285
  477.9 123.7 %reduce-scatter.20.cloned.1.call-start = ((), (), s32[]{:S(2)}) async-start(), calls=%async_computation.21 | async-start | bytes 2621440 | tf_op jit(solution)/shard_map/reduce_scatter | solution.py:291
  480.0 160.5 %reduce-scatter.12.cloned.1.call-start = ((), (), s32[]{:S(2)}) async-start(), calls=%async_computation.17 | async-start | bytes 2621440 | tf_op jit(solution)/shard_map/reduce_scatter | solution.py:279
  483.5 28.7 %copy-start.18 = (bf16[256,1024]{1,0:T(8,128)(2,1)S(1)}, bf16[256,1024]{1,0:T(8,128)(2,1)}, u32[]{:S(2)}) copy-start(bf16[256,1024]{1,0:T(8,128)(2,1)} %copy-done.17) | copy-start | bytes 1572868
  485.6 185.5 %reduce-scatter.14.cloned.1.call-start = ((), (), s32[]{:S(2)}) async-start(), calls=%async_computation.18 | async-start | bytes 1310720 | tf_op jit(solution)/shard_map/reduce_scatter | solution.py:282
  511.9 228.3 %reduce-scatter.22.cloned.1.call-start = ((), (), s32[]{:S(2)}) async-start(), calls=%async_computation.22 | async-start | bytes 7208960 | tf_op jit(solution)/shard_map/reduce_scatter | solution.py:297
  517.8 291.3 %reduce-scatter.24.cloned.1.call-start = ((), (), s32[]{:S(2)}) async-start(), calls=%async_computation.23 | async-start | bytes 7208960 | tf_op jit(solution)/shard_map/reduce_scatter | solution.py:300
  523.4 354.6 %reduce-scatter.26.cloned.1.call-start = ((), (), s32[]{:S(2)}) async-start(), calls=%async_computation.24 | async-start | bytes 7208960 | tf_op jit(solution)/shard_map/reduce_scatter | solution.py:303
  535.3 105.2 %copy-start.47 = (f32[256]{0:T(256)S(1)}, f32[256]{0:T(256)}, u32[]{:S(2)}) copy-start(f32[256]{0:T(256)} %copy-done.46) | copy-start | bytes 3076
  535.3 107.4 %copy-start.51 = (bf16[1024]{0:T(1024)(128)(2,1)S(1)}, bf16[1024]{0:T(1024)(128)(2,1)}, u32[]{:S(2)}) copy-start(bf16[1024]{0:T(1024)(128)(2,1)} %get-tuple-element.12) | copy-start | bytes 6148
  535.3 116.4 %copy-start.49 = (f32[256]{0:T(256)S(1)}, f32[256]{0:T(256)}, u32[]{:S(2)}) copy-start(f32[256]{0:T(256)} %copy-done.48) | copy-start | bytes 3076
  540.9 337.1 %copy-start.42 = (bf16[64,1024]{1,0:T(8,128)(2,1)S(1)}, bf16[64,1024]{1,0:T(8,128)(2,1)}, u32[]{:S(2)}) copy-start(bf16[64,1024]{1,0:T(8,128)(2,1)} %reduce-scatter.18.cloned.1.call-done) | copy-start | bytes 393220
  562.8 315.2 %copy-start.43 = (bf16[64,1024]{1,0:T(8,128)(2,1)S(1)}, bf16[64,1024]{1,0:T(8,128)(2,1)}, u32[]{:S(2)}) copy-start(bf16[64,1024]{1,0:T(8,128)(2,1)} %reduce-scatter.16.cloned.1.call-done) | copy-start | bytes 393220
  (27 other events, 85.9 us)
Sparse Core Ops, SparseCore 0:
  9.9 29.3 all-gather.11
  41.1 39.8 all-gather.9
  83.1 29.1 all-gather.13
  113.9 34.8 all-gather.15
  150.5 65.7 all-gather.17
  218.0 65.7 all-gather.19
  285.7 65.7 all-gather.21
  459.3 50.0 reduce-scatter.9
  512.1 22.9 reduce-scatter.17
  538.0 24.7 reduce-scatter.15
  566.4 35.1 reduce-scatter.19
  605.3 35.1 reduce-scatter.11
  643.4 27.7 reduce-scatter.13
  674.3 65.8 reduce-scatter.21
  743.2 65.7 reduce-scatter.23
  812.2 65.7 reduce-scatter.25
where the time goes:
time: 1130 us; the launch traced here: 1120 us
  waiting for transfers between devices  584 us (52%)
  blocking collectives  289 us (26%)
  matrix products  145 us (13%)
  local copies, waits for them, and re-layouts  51.7 us (5%)
  other arithmetic  26.2 us (2%)
  between operations  23.8 us (2%)
    psum x1, blocking collectives, per_device(): lax.psum((shares[0], shares[1], shares[2], shares[3], shares[4], shares[5...  236 us
    reduce_scatter x1, waiting for transfers between devices, per_device(): lax.psum_scatter(grads[7].astype(jnp.bfloat16), 'dp', scatter_dimension=0...  69 us
    reduce_scatter x1, waiting for transfers between devices, per_device(): lax.psum_scatter(grads[9].astype(jnp.bfloat16), 'dp', scatter_dimension=0...  68.9 us
    reduce_scatter x1, waiting for transfers between devices, per_device(): lax.psum_scatter(grads[8].astype(jnp.bfloat16), 'dp', scatter_dimension=0...  68.9 us
    all_gather x1, waiting for transfers between devices, per_device(): lax.all_gather(w_gate, 'dp', axis=0, tiled=True)  64.9 us
    all_gather x1, waiting for transfers between devices, per_device(): lax.all_gather(w_down, 'dp', axis=0, tiled=True)  61.8 us
    all_gather x1, waiting for transfers between devices, per_device(): lax.all_gather(w_up, 'dp', axis=0, tiled=True)  61.7 us
    reduce_scatter x1, waiting for transfers between devices, per_device(): lax.psum_scatter(grads[1].astype(jnp.bfloat16), 'dp', scatter_dimension=0...  38.9 us
  transfers between devices with their start and end apart: 16, of which 14 were waited for; matrix products, arithmetic and copies ran while one was open for 10% of the time, Pallas kernels for 0%

commit v1 on v0

--- a/solution.py
+++ b/solution.py
@@ -62,7 +62,9 @@
         lax.all_gather(w_value_up, "dp", axis=0, tiled=True),
         lax.all_gather(w_out, "dp", axis=0, tiled=True),
         lax.all_gather(norm2_gain, "dp", axis=0, tiled=True),
-        lax.all_gather(w_gate, "dp", axis=0, tiled=True),
+        jnp.concatenate(
+            lax.all_to_all(jnp.stack([w_gate] * lax.axis_size("dp")), "dp", 0, 0), axis=0
+        ),
         lax.all_gather(w_up, "dp", axis=0, tiled=True),
         lax.all_gather(w_down, "dp", axis=0, tiled=True),
     )

time: 1130 us -> 1110 us (0.982)
  waiting for transfers between devices: 584 us -> 493 us
  blocking collectives: 289 us -> 354 us
    all_gather x1, blocking collectives: 14 us -> 82.4 us  [per_device(): lax.all_gather(w_key_up, 'dp', axis=0, tiled=True)]
    all_gather x1 -> x0, waiting for transfers between devices: 64.9 us -> none  [per_device(): lax.all_gather(w_gate, 'dp', axis=0, tiled=True)]
    all_gather x1, waiting for transfers between devices: 18 us -> 0.02 us  [per_device(): lax.all_gather(latent_pieces, 'seq', axis=1, tiled=True)]
  transfers between devices with their start and end apart: 16 -> 16, of which waited for: 14 -> 12; matrix products, arithmetic and copies ran while one was open for 10% -> 10% of each run, Pallas kernels for 0% -> 0%
where the time goes in v1:
time: 1110 us; the launch traced here: 1100 us
  waiting for transfers between devices  493 us (44%)
  blocking collectives  354 us (32%)
  matrix products  145 us (13%)
  local copies, waits for them, and re-layouts  55.4 us (5%)
  other arithmetic  26.3 us (2%)
  between operations  23.8 us (2%)
    psum x1, blocking collectives, per_device(): lax.psum((shares[0], shares[1], shares[2], shares[3], shares[4], shares[5...  236 us
    all_gather x1, blocking collectives, per_device(): lax.all_gather(w_key_up, 'dp', axis=0, tiled=True)  82.4 us
    reduce_scatter x1, waiting for transfers between devices, per_device(): lax.psum_scatter(grads[7].astype(jnp.bfloat16), 'dp', scatter_dimension=0...  69.1 us
    reduce_scatter x1, waiting for transfers between devices, per_device(): lax.psum_scatter(grads[8].astype(jnp.bfloat16), 'dp', scatter_dimension=0...  68.9 us
    reduce_scatter x1, waiting for transfers between devices, per_device(): lax.psum_scatter(grads[9].astype(jnp.bfloat16), 'dp', scatter_dimension=0...  68.9 us
    all_gather x1, waiting for transfers between devices, per_device(): lax.all_gather(w_down, 'dp', axis=0, tiled=True)  61.7 us
    all_gather x1, waiting for transfers between devices, per_device(): lax.all_gather(w_up, 'dp', axis=0, tiled=True)  58.7 us
    reduce_scatter x1, waiting for transfers between devices, per_device(): lax.psum_scatter(grads[1].astype(jnp.bfloat16), 'dp', scatter_dimension=0...  39 us
  transfers between devices with their start and end apart: 16, of which 12 were waited for; matrix products, arithmetic and copies ran while one was open for 10% of the time, Pallas kernels for 0%

profile of v1, /device:TPU:0, one launch (start us, length us, event | category | flops | bytes accessed | tf_op | source)
XLA Modules:
  0.0 1104.0 jit_solution(16555868787294143053)
XLA Ops:
  11.3 9.5 all-gather
  22.6 16.6 %all-gather.11.cloned.1.call-done = bf16[1024,512]{1,0:T(8,128)(2,1)} async-done(((bf16[256,512]{1,0:T(8,128)(2,1)}), bf16[1024,512]{1,0:T(8,128)(2,1)}) %all-gather.11.cloned.1.call-update) | async-done | bytes 1048592 | tf_op jit(solution)/shard_map/all_gather | solution.py:60
  45.6 5.4 all-to-all-start
  53.8 82.4 %all_gather.33 = bf16[256,1024]{1,0:T(8,128)(2,1)S(1)} all-gather(bf16[64,1024]{1,0:T(8,128)(2,1)S(1)} %copy-done.41), channel_id=1, replica_groups=mesh['dp'=4,'seq'=8] {'dp'}, dimensions={0}, use_global_device_ids=true | all-gather | bytes 655360 | tf_op jit(solution)/shard_map/all_gather | solution.py:61
  136.7 9.4 all_gather.36
  152.6 8.2 all-gather.1
  166.9 4.0 dynamic-slice_bitcast_fusion.3
  171.6 3.1 fusion.67
  177.8 3.2 fusion.66
  184.1 3.3 fusion.32
  187.4 3.5 fusion.29
  195.7 4.1 all-gather.15.cloned.1.call-done
  202.5 6.2 fusion.68
  208.7 58.7 %all-gather.17.cloned.1.call-done = bf16[1024,2816]{1,0:T(8,128)(2,1)} async-done(((bf16[256,2816]{1,0:T(8,128)(2,1)}), bf16[1024,2816]{1,0:T(8,128)(2,1)}) %all-gather.17.cloned.1.call-update) | async-done | bytes 5767184 | tf_op jit(solution)/shard_map/all_gather | solution.py:68
  267.4 5.9 fusion.69
  273.2 61.7 %all-gather.19.cloned.1.call-done = bf16[2816,1024]{1,0:T(8,128)(2,1)} async-done(((bf16[704,1024]{1,0:T(8,128)(2,1)}), bf16[2816,1024]{1,0:T(8,128)(2,1)}) %all-gather.19.cloned.1.call-update) | async-done | bytes 5767184 | tf_op jit(solution)/shard_map/all_gather | solution.py:69
  334.9 9.5 multiply_convert_fusion.2
  344.4 5.4 fusion.70
  354.5 5.3 multiply_reduce_fusion
  361.3 6.8 multiply_convert_fusion
  370.3 4.0 fusion.49
  374.3 8.1 bitcast_add_fusion
  382.5 6.1 multiply_convert_fusion.1
  390.7 4.0 fusion.52
  394.8 7.5 bitcast_add_fusion.1
  402.2 3.0 fusion.11
  407.7 6.7 dynamic_update_slice.12
  417.2 6.5 dynamic_update_slice.13
  426.5 6.5 dynamic_update_slice.14
  435.8 6.6 dynamic_update_slice.15
  442.4 4.5 convolution_convert_fusion.8
  448.1 4.7 fusion.55
  452.8 4.6 fusion.56
  468.9 23.6 %reduce-scatter.10.cloned.1.call-done = f32[4,64,512]{2,1,0:T(8,128)} async-done(((f32[4,512,512]{2,1,0:T(8,128)}), f32[4,64,512]{2,1,0:T(8,128)}) %reduce-scatter.10.cloned.1.call-update) | async-done | bytes 524304 | tf_op jit(solution)/shard_map/reduce_scatter | solution.py:241
  495.4 5.6 convolution_convert_fusion.2
  501.1 5.6 convolution_convert_fusion.1
  508.0 5.2 convolution_convert_fusion
  515.1 3.5 fusion.71
  518.6 5.6 fusion.21
  524.2 22.0 %reduce-scatter.16.cloned.1.call-done = bf16[64,1024]{1,0:T(8,128)(2,1)} async-done(((bf16[256,1024]{1,0:T(8,128)(2,1)}), bf16[64,1024]{1,0:T(8,128)(2,1)}) %reduce-scatter.16.cloned.1.call-update) | async-done | bytes 131088 | tf_op jit(solution)/shard_map/reduce_scatter | solution.py:287
  546.2 38.6 %reduce-scatter.20.cloned.1.call-done = bf16[256,1024]{1,0:T(8,128)(2,1)} async-done(((bf16[1024,1024]{1,0:T(8,128)(2,1)}), bf16[256,1024]{1,0:T(8,128)(2,1)}) %reduce-scatter.20.cloned.1.call-update) | async-done | bytes 524304 | tf_op jit(solution)/shard_map/reduce_scatter | solution.py:293
  584.8 39.0 %reduce-scatter.12.cloned.1.call-done = bf16[256,1024]{1,0:T(8,128)(2,1)} async-done(((bf16[1024,1024]{1,0:T(8,128)(2,1)}), bf16[256,1024]{1,0:T(8,128)(2,1)}) %reduce-scatter.12.cloned.1.call-update) | async-done | bytes 524304 | tf_op jit(solution)/shard_map/reduce_scatter | solution.py:281
  626.0 8.9 all-reduce.3
  636.2 18.1 %reduce-scatter.14.cloned.1.call-done = bf16[256,512]{1,0:T(8,128)(2,1)} async-done(((bf16[1024,512]{1,0:T(8,128)(2,1)}), bf16[256,512]{1,0:T(8,128)(2,1)}) %reduce-scatter.14.cloned.1.call-update) | async-done | bytes 262160 | tf_op jit(solution)/shard_map/reduce_scatter | solution.py:284
  654.3 69.1 %reduce-scatter.22.cloned.1.call-done = bf16[256,2816]{1,0:T(8,128)(2,1)} async-done(((bf16[1024,2816]{1,0:T(8,128)(2,1)}), bf16[256,2816]{1,0:T(8,128)(2,1)}) %reduce-scatter.22.cloned.1.call-update) | async-done | bytes 1441808 | tf_op jit(solution)/shard_map/reduce_scatter | solution.py:299
  723.4 68.9 %reduce-scatter.24.cloned.1.call-done = bf16[256,2816]{1,0:T(8,128)(2,1)} async-done(((bf16[1024,2816]{1,0:T(8,128)(2,1)}), bf16[256,2816]{1,0:T(8,128)(2,1)}) %reduce-scatter.24.cloned.1.call-update) | async-done | bytes 1441808 | tf_op jit(solution)/shard_map/reduce_scatter | solution.py:302
  792.4 68.9 %reduce-scatter.26.cloned.1.call-done = bf16[704,1024]{1,0:T(8,128)(2,1)} async-done(((bf16[2816,1024]{1,0:T(8,128)(2,1)}), bf16[704,1024]{1,0:T(8,128)(2,1)}) %reduce-scatter.26.cloned.1.call-update) | async-done | bytes 1441808 | tf_op jit(solution)/shard_map/reduce_scatter | solution.py:305
  861.3 235.7 %all-reduce.5 = (f32[256]{0:T(256)}, f32[256,1024]{1,0:T(8,128)}, f32[256,512]{1,0:T(8,128)}, f32[64,1024]{1,0:T(8,128)}, f32[64,1024]{1,0:T(8,128)}, /*index=5*...) all-reduce(f32[256]{0:T(256)S(1)} %get-tuple-element.60, ...), channel_id=1, replica_groups=mesh['dp'=4,'seq'=8] {'seq'}, use_global_device_ids=true, to_apply=%region_15.16 | all-reduce | flops 2949632 | bytes 17698816 | tf_op jit(solution)/shard_map/psum | solution.py:309
  (230 shorter events, 76.7 us)
Async XLA Ops:
  7.2 35.6 %copy-start.36 = (bf16[256,2816]{1,0:T(8,128)(2,1)S(1)}, bf16[256,2816]{1,0:T(8,128)(2,1)}, u32[]{:S(2)}) copy-start(bf16[256,2816]{1,0:T(8,128)(2,1)} %param.21) | copy-start | bytes 4325380
  7.2 32.0 %all-gather.11.cloned.1.call-start = ((), (), s32[]{:S(2)}) async-start(), calls=%async_computation.11 | async-start | bytes 1310720 | tf_op jit(solution)/shard_map/all_gather | solution.py:60
  7.9 155.5 %all-gather.9.cloned.1.call-start = ((), (), s32[]{:S(2)}) async-start(), calls=%async_computation.10 | async-start | bytes 2621440 | tf_op jit(solution)/shard_map/all_gather | solution.py:59
  8.7 158.2 %all-gather.13.cloned.1.call-start = ((), (), s32[]{:S(2)}) async-start(), calls=%async_computation.12 | async-start | bytes 2359296 | tf_op jit(solution)/shard_map/all_gather | solution.py:127
  10.6 10.2 copy-start.49
  10.6 10.2 copy-start.47
  41.6 158.2 %all-gather.15.cloned.1.call-start = ((), (), s32[]{:S(2)}) async-start(), calls=%async_computation.13 | async-start | bytes 2621440 | tf_op jit(solution)/shard_map/all_gather | solution.py:63
  42.2 225.2 %all-gather.17.cloned.1.call-start = ((), (), s32[]{:S(2)}) async-start(), calls=%async_computation.14 | async-start | bytes 7208960 | tf_op jit(solution)/shard_map/all_gather | solution.py:68
  45.6 7.0 copy-start.53
  45.6 8.1 copy-start.41
  45.6 91.1 %copy-start.42 = (bf16[64,1024]{1,0:T(8,128)(2,1)S(1)}, bf16[64,1024]{1,0:T(8,128)(2,1)}, u32[]{:S(2)}) copy-start(bf16[64,1024]{1,0:T(8,128)(2,1)} %param.18) | copy-start | bytes 393220
  45.6 156.8 %all-to-all-start = ((bf16[4,256,2816]{2,1,0:T(8,128)(2,1)}), bf16[4,256,2816]{2,1,0:T(8,128)(2,1)}, u32[]{:S(2)}, u32[]{:S(2)}) async-start(bf16[4,256,2816]{2,1,0:T(8,128)(2,1)} %stack.32), calls=%async_computation | async-start | bytes 11534336 | tf_op jit(solution)/shard_map/all_to_all | solution.py:66
  51.0 101.5 %copy-start.55 = (bf16[256]{0:T(256)(128)(2,1)S(1)}, bf16[256]{0:T(256)(128)(2,1)}, u32[]{:S(2)}) copy-start(bf16[256]{0:T(256)(128)(2,1)} %param.20) | copy-start | bytes 1540
  51.1 283.8 %all-gather.19.cloned.1.call-start = ((), (), s32[]{:S(2)}) async-start(), calls=%async_computation.15 | async-start | bytes 7208960 | tf_op jit(solution)/shard_map/all_gather | solution.py:69
  51.6 440.9 %reduce-scatter.10.cloned.1.call-start = ((), (), s32[]{:S(2)}) async-start(), calls=%async_computation.16 | async-start | bytes 4718592 | tf_op jit(solution)/shard_map/reduce_scatter | solution.py:241
  151.5 15.1 %copy-start.29 = (bf16[256,1024]{0,1:T(8,128)(2,1)}, bf16[256,1024]{0,1:T(8,128)(2,1)S(1)}, u32[]{:S(2)}) copy-start(bf16[256,1024]{0,1:T(8,128)(2,1)S(1)} %copy.133) | copy-start | bytes 1572868
  166.9 10.9 copy-start.39
  171.6 6.2 copy-start.3
  174.7 9.3 copy-start
  181.0 6.4 copy-start.1
  191.0 8.9 copy-start.5
  195.7 13.0 %copy-start.26 = (bf16[16,256,64]{1,2,0:T(8,128)(2,1)}, bf16[16,256,64]{1,2,0:T(8,128)(2,1)S(1)}, u32[]{:S(2)}) copy-start(bf16[16,256,64]{1,2,0:T(8,128)(2,1)S(1)} %convolution_convert_fusion.10) | copy-start | bytes 1572868
  202.3 150.0 %copy-start.11 = (f32[256,1024]{1,0:T(8,128)}, f32[256,1024]{1,0:T(8,128)S(1)}, u32[]{:S(2)}) copy-start(f32[256,1024]{1,0:T(8,128)S(1)} %get-tuple-element.54) | copy-start | bytes 3145732
  202.4 64.9 %copy-start.17 = (bf16[256,1024]{1,0:T(8,128)(2,1)}, bf16[256,1024]{1,0:T(8,128)(2,1)S(1)}, u32[]{:S(2)}) copy-start(bf16[256,1024]{1,0:T(8,128)(2,1)S(1)} %multiply_convert_fusion.4) | copy-start | bytes 1572868
  208.7 126.2 %copy-start.31 = (bf16[1,4,64,1024]{3,2,1,0:T(8,128)(2,1)S(1)}, bf16[1,4,64,1024]{3,2,1,0:T(8,128)(2,1)}, u32[]{:S(2)}) copy-start(bf16[1,4,64,1024]{3,2,1,0:T(8,128)(2,1)} %param.24) | copy-start | bytes 1572868
  361.0 7.0 copy-start.16
  361.2 9.0 copy-start.40
  370.3 12.2 %slice-start = ((s8[9437184]{0:T(1024)(128)(4,1)}), s8[4194304]{0:T(1024)(128)(4,1)S(1)}, s32[]{:S(2)}) async-start(s8[9437184]{0:T(1024)(128)(4,1)} %bitcast.167), calls=%async_computation.25 | async-start | bytes 8388608
  370.3 12.2 %slice-start.1 = ((s8[9437184]{0:T(1024)(128)(4,1)}), s8[4194304]{0:T(1024)(128)(4,1)S(1)}, s32[]{:S(2)}) async-start(s8[9437184]{0:T(1024)(128)(4,1)} %bitcast.167), calls=%async_computation.26 | async-start | bytes 8388608
  374.3 8.2 slice-start.2
  374.3 8.2 copy-start.32
  382.4 19.8 %copy-start.2 = (f32[4,1088,256]{2,1,0:T(8,128)}, f32[4,1088,256]{2,1,0:T(8,128)S(1)}, u32[]{:S(2)}) copy-start(f32[4,1088,256]{2,1,0:T(8,128)S(1)} %bitcast_add_fusion) | copy-start | bytes 13369348
  382.5 8.2 copy-start.38
  435.8 6.7 copy-start.20
  442.4 81.8 %reduce-scatter.18.cloned.1.call-start = ((), (), s32[]{:S(2)}) async-start(), calls=%async_computation.20 | async-start | bytes 655360 | tf_op jit(solution)/shard_map/reduce_scatter | solution.py:290
  448.0 98.2 %reduce-scatter.16.cloned.1.call-start = ((), (), s32[]{:S(2)}) async-start(), calls=%async_computation.19 | async-start | bytes 655360 | tf_op jit(solution)/shard_map/reduce_scatter | solution.py:287
  461.1 123.6 %reduce-scatter.20.cloned.1.call-start = ((), (), s32[]{:S(2)}) async-start(), calls=%async_computation.21 | async-start | bytes 2621440 | tf_op jit(solution)/shard_map/reduce_scatter | solution.py:293
  463.3 160.6 %reduce-scatter.12.cloned.1.call-start = ((), (), s32[]{:S(2)}) async-start(), calls=%async_computation.17 | async-start | bytes 2621440 | tf_op jit(solution)/shard_map/reduce_scatter | solution.py:281
  466.7 28.7 %copy-start.18 = (bf16[256,1024]{1,0:T(8,128)(2,1)S(1)}, bf16[256,1024]{1,0:T(8,128)(2,1)}, u32[]{:S(2)}) copy-start(bf16[256,1024]{1,0:T(8,128)(2,1)} %copy-done.17) | copy-start | bytes 1572868
  468.8 185.5 %reduce-scatter.14.cloned.1.call-start = ((), (), s32[]{:S(2)}) async-start(), calls=%async_computation.18 | async-start | bytes 1310720 | tf_op jit(solution)/shard_map/reduce_scatter | solution.py:284
  495.1 228.3 %reduce-scatter.22.cloned.1.call-start = ((), (), s32[]{:S(2)}) async-start(), calls=%async_computation.22 | async-start | bytes 7208960 | tf_op jit(solution)/shard_map/reduce_scatter | solution.py:299
  501.0 291.4 %reduce-scatter.24.cloned.1.call-start = ((), (), s32[]{:S(2)}) async-start(), calls=%async_computation.23 | async-start | bytes 7208960 | tf_op jit(solution)/shard_map/reduce_scatter | solution.py:302
  506.7 354.7 %reduce-scatter.26.cloned.1.call-start = ((), (), s32[]{:S(2)}) async-start(), calls=%async_computation.24 | async-start | bytes 7208960 | tf_op jit(solution)/shard_map/reduce_scatter | solution.py:305
  518.6 105.3 %copy-start.48 = (f32[256]{0:T(256)S(1)}, f32[256]{0:T(256)}, u32[]{:S(2)}) copy-start(f32[256]{0:T(256)} %copy-done.47) | copy-start | bytes 3076
  518.6 107.4 %copy-start.52 = (bf16[1024]{0:T(1024)(128)(2,1)S(1)}, bf16[1024]{0:T(1024)(128)(2,1)}, u32[]{:S(2)}) copy-start(bf16[1024]{0:T(1024)(128)(2,1)} %get-tuple-element.12) | copy-start | bytes 6148
  518.6 116.5 %copy-start.50 = (f32[256]{0:T(256)S(1)}, f32[256]{0:T(256)}, u32[]{:S(2)}) copy-start(f32[256]{0:T(256)} %copy-done.49) | copy-start | bytes 3076
  524.2 337.2 %copy-start.43 = (bf16[64,1024]{1,0:T(8,128)(2,1)S(1)}, bf16[64,1024]{1,0:T(8,128)(2,1)}, u32[]{:S(2)}) copy-start(bf16[64,1024]{1,0:T(8,128)(2,1)} %reduce-scatter.18.cloned.1.call-done) | copy-start | bytes 393220
  546.2 315.1 %copy-start.44 = (bf16[64,1024]{1,0:T(8,128)(2,1)S(1)}, bf16[64,1024]{1,0:T(8,128)(2,1)}, u32[]{:S(2)}) copy-start(bf16[64,1024]{1,0:T(8,128)(2,1)} %reduce-scatter.16.cloned.1.call-done) | copy-start | bytes 393220
  (28 other events, 83.7 us)
Sparse Core Ops, SparseCore 0:
  9.9 29.3 all-gather.10
  41.1 80.4 all-gather.8
  123.8 39.4 all-gather.12
  165.0 34.7 all-gather.14
  201.5 65.7 all-gather.16
  269.1 65.7 all-gather.18
  442.5 50.0 reduce-scatter.9
  495.4 22.9 reduce-scatter.17
  521.4 24.7 reduce-scatter.15
  549.6 35.1 reduce-scatter.19
  588.6 35.1 reduce-scatter.11
  626.6 27.6 reduce-scatter.13
  657.6 65.8 reduce-scatter.21
  726.6 65.7 reduce-scatter.23
  795.5 65.7 reduce-scatter.25
